TPU v7x, 32 devices: a whole 2x2x4 slice. The times are simulated.
32 devices in a mesh: group: 1, tile: 8 (over z, core), dp: 4 (over y, x).
Axes of the slice: x: 2, y: 2, z: 4, core: 2. Of those that a mesh axis runs over, the one named last changes fastest.
Arguments:
- activations: bfloat16 [4, 8, 24, 24, 128], P(('group', 'dp'), 'tile'), may hold values from -6 to 6
- cotangent: bfloat16 [4, 8, 24, 24, 128], P(('group', 'dp'), 'tile'), may hold values from -1.5 to 1.5
- kernel: bfloat16 [1152, 128], P('group'), may hold values from -0.1875 to 0.1875
- turning: int32 [8], P('tile'), may hold values from 0 to 3
- orient: int32 [8, 4], P('tile'), may hold values from 0 to 7, as said below
- left_factor: float32 [1152, 1152], P(('group', 'tile')), may hold values from -0.15 to 5.15
- left_basis: float32 [1152, 1152], P(('group', 'tile'), 'dp'), may hold values from -0.026516504 to 1.0265165
- right_factor: float32 [128, 128], P('group'), may hold values from -4.26 to 49.26
- right_basis: float32 [128, 128], P('group'), may hold values from -0.079549513 to 1.0795495
- momentum: float32 [1152, 128], P(('group', 'dp')), may hold values from -1.5 to 1.5
- second_moment: float32 [1152, 128], P(('group', 'dp')), may hold values from 0.02 to 0.2
Outputs:
- output: bfloat16 [4, 8, 24, 24, 128], P(('group', 'dp'), 'tile')
- input_grad: bfloat16 [4, 8, 24, 24, 128], P(('group', 'dp'), 'tile')
- kernel_grad: float32 [1152, 128], P('group')
- left_factor_new: float32 [1152, 1152], P(('group', 'tile'))
- left_basis_new: float32 [1152, 1152], P(('group', 'tile'))
- right_factor_new: float32 [128, 128], P('group')
- right_basis_new: float32 [128, 128], P('group')
- momentum_new: float32 [1152, 128], P(('group', 'dp'))
- second_new: float32 [1152, 128], P(('group', 'dp'))
- update: float32 [1152, 128], P(('group', 'tile'))
Inputs may be any that keep to these rules, and one draw needn't show every extreme that they name: 0 where edge e of tile t leaves the patch; otherwise orient[t, e] % 4 is the edge of neighbor[t, e] that heads back to t, and 4 is added where the two edges' cell orders run opposite ways.
All inputs are finite; a program needn't handle non-finite values.
Results may differ from a plain program's by a relative error of at most 0.0025.
Values may be sent and summed in bfloat16 or wider, within the bound.
A program may use at most 128 MiB of HBM per device.

v0:
```python
import math
import jax
import jax.numpy as jnp
from jax import lax
from jax.sharding import PartitionSpec as P

highest = lax.Precision.HIGHEST
epsilon = 1e-08


def edge_strips(values):
    return jnp.stack(
        [values[..., 0, :, :], values[..., :, -1, :], values[..., -1, :, :], values[..., :, 0, :]],
        axis=0,
    )


def cycle_strips(spread):
    return jnp.stack(
        [spread[:, 0, 1:-1], spread[:, 1:-1, -1], spread[:, -1, 1:-1], spread[:, 1:-1, 0]], axis=0
    )


def assemble(tile_vals, borders):
    middle = jnp.concatenate(
        [borders[3][:, :, None, :], tile_vals, borders[1][:, :, None, :]], axis=2
    )
    top_row = jnp.pad(borders[0], ((0, 0), (1, 1), (0, 0)))[:, None]
    bottom_row = jnp.pad(borders[2], ((0, 0), (1, 1), (0, 0)))[:, None]
    return jnp.concatenate([top_row, middle, bottom_row], axis=1)


def tap_patches(padded, side):
    pieces = [
        padded[:, row_off : row_off + side, col_off : col_off + side, :]
        for row_off in range(3)
        for col_off in range(3)
    ]
    joined = jnp.concatenate(pieces, axis=-1)
    return joined.reshape(-1, joined.shape[-1])


def spread_back(flat_grads, kernel, sample_count, side):
    channels = kernel.shape[1]
    summed = jnp.zeros((sample_count, side + 2, side + 2, channels), jnp.float32)
    for tap_index in range(9):
        row_off, col_off = divmod(tap_index, 3)
        weight_tap = kernel[tap_index * channels : (tap_index + 1) * channels]
        contrib = lax.dot_general(
            flat_grads, weight_tap, (((1,), (1,)), ((), ())), preferred_element_type=jnp.float32
        )
        contrib = contrib.reshape(sample_count, side, side, channels)
        summed = summed + jnp.pad(
            contrib, ((0, 0), (row_off, 2 - row_off), (col_off, 2 - col_off), (0, 0))
        )
    return summed


def absorb_rims(interior, incoming):
    result = interior.at[..., 0, :, :].add(incoming[0])
    result = result.at[..., :, -1, :].add(incoming[1])
    result = result.at[..., -1, :, :].add(incoming[2])
    return result.at[..., :, 0, :].add(incoming[3])


def flip_edges(strips, flipped):
    return jnp.where(flipped[:, None, None, None], strips[:, :, ::-1, :], strips)


def pick_gathered(everything, near_tiles, facing, flipped, usable):
    flat = everything.reshape(everything.shape[0] * 4, -1)
    wanted = jnp.where(usable, near_tiles * 4 + facing, -1)
    selector = (lax.broadcasted_iota(jnp.int32, (4, flat.shape[0]), 1) == wanted[:, None]).astype(
        jnp.bfloat16
    )
    picked = jnp.dot(selector, flat, preferred_element_type=jnp.float32).astype(jnp.bfloat16)
    return flip_edges(picked.reshape((4,) + everything.shape[2:]), flipped)


def orthonormal(power):
    gram = lax.dot_general(power, power, (((0,), (0,)), ((), ())), precision=highest)
    lower = jnp.linalg.cholesky(gram)
    return lax.linalg.triangular_solve(lower, power.T, left_side=True, lower=True).T


def body(
    activations,
    cotangent,
    kernel,
    turning,
    orient,
    left_factor,
    left_basis,
    right_factor,
    right_basis,
    momentum,
    second_moment,
):
    tiles = lax.axis_size("tile")
    dp_count = lax.axis_size("dp")
    tile_index = lax.axis_index("tile")
    dp_index = lax.axis_index("dp")
    tile_vals = activations[:, 0]
    tile_grads = cotangent[:, 0]
    sample_count = tile_vals.shape[0]
    side = tile_vals.shape[1]
    channels = tile_vals.shape[-1]
    own_turn = turning[0]
    facing = orient[0] % 4
    flipped = orient[0] >= 4
    heading = (jnp.arange(4, dtype=jnp.int32) + own_turn) % 4
    row_of = tile_index // 4
    col_of = tile_index % 4
    room = jnp.stack([row_of > 0, col_of < 3, row_of < tiles // 4 - 1, col_of > 0])
    usable = (
        jnp.sum(
            jnp.where(
                heading[:, None] == jnp.arange(4, dtype=jnp.int32)[None, :], room[None, :], False
            ),
            axis=1,
        )
        > 0
    )
    offsets = jnp.array([-4, 1, 4, -1], dtype=jnp.int32)
    near_tiles = tile_index + jnp.sum(
        jnp.where(heading[:, None] == jnp.arange(4, dtype=jnp.int32)[None, :], offsets[None, :], 0),
        axis=1,
    )
    strips = edge_strips(tile_vals)
    everything = lax.all_gather(strips[None], "tile", axis=0, tiled=True)
    borders = pick_gathered(everything, near_tiles, facing, flipped, usable)
    padded = assemble(tile_vals, borders)
    columns = tap_patches(padded, side)
    flat_grads = tile_grads.reshape(-1, channels)
    partial_grad = lax.dot_general(
        columns, flat_grads, (((0,), (0,)), ((), ())), preferred_element_type=jnp.float32
    )
    summed_grad = lax.psum(partial_grad, ("tile", "dp"))
    result = jnp.dot(columns, kernel, preferred_element_type=jnp.float32).astype(jnp.bfloat16)
    result = result.reshape(activations.shape)
    spread = spread_back(flat_grads, kernel, sample_count, side)
    rim_cells = cycle_strips(spread).astype(jnp.bfloat16)
    all_rims = lax.all_gather(rim_cells[None], "tile", axis=0, tiled=True)
    incoming = pick_gathered(all_rims, near_tiles, facing, flipped, usable)
    input_grad = absorb_rims(spread[:, 1:-1, 1:-1], incoming.astype(jnp.float32)).astype(
        jnp.bfloat16
    )
    input_grad = input_grad.reshape(cotangent.shape)
    cells = dp_count * sample_count * tiles * side * side
    grad = summed_grad * (1.0 / math.sqrt(cells))
    rows_per = left_factor.shape[0]
    width = left_factor.shape[1]
    cols_per = left_basis.shape[1]
    col_start = dp_index * cols_per
    grad_rows = lax.dynamic_slice_in_dim(grad, tile_index * rows_per, rows_per, 0)
    left_new = 0.95 * left_factor + 0.05 * lax.dot_general(
        grad_rows, grad, (((1,), (1,)), ((), ())), precision=highest
    )
    basis_rows = lax.all_gather(left_basis, "dp", axis=1, tiled=True)
    power = jnp.zeros((rows_per, width), jnp.float32) + jnp.dot(
        left_new,
        lax.all_gather(basis_rows.astype(jnp.bfloat16), "tile", axis=0, tiled=True).astype(
            jnp.float32
        ),
        precision=highest,
    )
    power_cols = lax.dynamic_slice_in_dim(power, col_start, cols_per, 1)
    gram_part = lax.psum(
        lax.dot_general(power, power_cols, (((0,), (0,)), ((), ())), precision=highest), "tile"
    )
    gram = lax.all_gather(gram_part, "dp", axis=1, tiled=True)
    lower = jnp.linalg.cholesky(gram)
    basis_new = lax.linalg.triangular_solve(lower, power.T, left_side=True, lower=True).T
    right_new = 0.95 * right_factor + 0.05 * lax.dot_general(
        grad, grad, (((0,), (0,)), ((), ())), precision=highest
    )
    right_basis_new = orthonormal(jnp.dot(right_new, right_basis, precision=highest))
    back = lax.psum(jnp.dot(left_basis, momentum, precision=highest), "dp")
    basis_cols = lax.dynamic_slice_in_dim(basis_new, col_start, cols_per, 1)
    turned_momentum, turned_grad = lax.psum(
        (
            lax.dot_general(basis_cols, back, (((0,), (0,)), ((), ())), precision=highest),
            lax.dot_general(basis_cols, grad_rows, (((0,), (0,)), ((), ())), precision=highest),
        ),
        "tile",
    )
    right_turn = lax.dot_general(
        right_basis, right_basis_new, (((0,), (0,)), ((), ())), precision=highest
    )
    rotated = jnp.dot(turned_momentum, right_turn, precision=highest)
    projected = jnp.dot(turned_grad, right_basis_new, precision=highest)
    momentum_new = 0.9 * rotated + 0.1 * projected
    second_new = 0.95 * second_moment + 0.05 * projected * projected
    normalized = momentum_new / (jnp.sqrt(second_new) + epsilon)
    whole_moment = lax.all_gather(normalized, "dp", axis=0, tiled=True)
    update_rows = jnp.dot(basis_new, whole_moment, precision=highest)
    update = lax.dot_general(
        update_rows, right_basis_new, (((1,), (1,)), ((), ())), precision=highest
    )
    return (
        result,
        input_grad,
        grad,
        left_new,
        basis_new,
        right_new,
        right_basis_new,
        momentum_new,
        second_new,
        update,
    )


def solution(mesh):
    placed = (
        P(("group", "dp"), "tile", None, None, None),
        P(("group", "dp"), "tile", None, None, None),
        P("group", None),
        P("tile"),
        P("tile", None),
        P(("group", "tile"), None),
        P(("group", "tile"), "dp"),
        P("group", None),
        P("group", None),
        P(("group", "dp"), None),
        P(("group", "dp"), None),
    )
    return jax.shard_map(
        body,
        mesh=mesh,
        in_specs=placed,
        out_specs=(
            P(("group", "dp"), "tile", None, None, None),
            P(("group", "dp"), "tile", None, None, None),
            P("group", None),
            P(("group", "tile"), None),
            P(("group", "tile"), None),
            P("group", None),
            P("group", None),
            P(("group", "dp"), None),
            P(("group", "dp"), None),
            P(("group", "tile"), None),
        ),
        check_vma=False,
    )
```

profile of v0, /device:TPU:0, one launch (start us, length us, event | category | flops | bytes accessed | tf_op | source)
XLA Modules:
  0.0 795.9 jit_solution(18225096363000132094)
XLA Ops:
  19.2 15.8 %all_gather.19 = bf16[8,4,1,24,128]{4,3,2,1,0:T(8,128)(2,1)S(1)} all-gather(bf16[1,4,1,24,128]{4,3,2,1,0:T(8,128)(2,1)S(1)} %pad_maximum_fusion.4), channel_id=1, replica_groups=mesh['group'=1,'tile'=8,'dp'=4] {'tile'}, dimensions={0}, use_global_device_ids=true | all-gather | bytes 221184 | tf_op jit(solution)/shard_map/all_gather | solution.py:143
  36.3 14.1 %all-gather = bf16[32,1,24,128]{3,2,1,0:T(8,128)(2,1)S(1)} all-gather(bf16[4,1,24,128]{3,2,1,0:T(8,128)(2,1)S(1)} %pad_maximum_fusion.3), channel_id=2, replica_groups=mesh['group'=1,'tile'=8,'dp'=4] {'tile'}, dimensions={0}, use_global_device_ids=true | all-gather | bytes 221184 | tf_op jit(solution)/shard_map/all_gather | solution.py:130
  53.1 10.2 %all-gather.1 = bf16[4,288,144]{1,2,0:T(8,128)(2,1)S(1)} all-gather(bf16[1,288,144]{1,2,0:T(8,128)(2,1)S(1)} %bitcast_convert_fusion), channel_id=1, replica_groups=mesh['group'=1,'tile'=8,'dp'=4] {'dp'}, dimensions={0}, use_global_device_ids=true | all-gather | bytes 414720 | tf_op jit(solution)/shard_map/all_gather | solution.py:159
  64.7 132.0 %all-reduce.18.cloned.1.call-done = f32[1152,128]{1,0:T(8,128)} async-done(((f32[1152,128]{1,0:T(8,128)}), f32[1152,128]{1,0:T(8,128)}) %all-reduce.18.cloned.1.call-update) | async-done | bytes 589840 | tf_op jit(solution)/shard_map/psum | solution.py:138
  206.1 60.6 %all-reduce.20.cloned.1.call-done = f32[1152,288]{0,1:T(8,128)} async-done(((f32[1152,288]{0,1:T(8,128)}), f32[1152,288]{0,1:T(8,128)}) %all-reduce.20.cloned.1.call-update) | async-done | bytes 1327120 | tf_op jit(solution)/shard_map/psum | solution.py:168
  276.5 11.7 %cholesky.693 = f32[128,128]{1,0:T(8,128)S(1)} custom-call(f32[128,128]{1,0:T(8,128)S(1)} %fusion.98), custom_call_target="Cholesky" | custom-call | tf_op jit(solution)/shard_map/jit(cholesky)/cholesky | solution.py:82
  289.6 9.8 %custom-call.85 = f32[1,128,128]{1,2,0:T(8,128)S(1)} custom-call(f32[1,128,128]{2,1,0:T(8,128)S(1)} %fusion.85), custom_call_target="InvertDiagBlocksLowerTriangular" | custom-call | tf_op jit(solution)/shard_map/triangular_solve | solution.py:83
  300.4 28.1 %all-gather.7.cloned.1.call-done = f32[1152,1152]{0,1:T(8,128)} async-done(((f32[1152,288]{0,1:T(8,128)}), f32[1152,1152]{0,1:T(8,128)}) %all-gather.7.cloned.1.call-update) | async-done | bytes 5308432 | tf_op jit(solution)/shard_map/all_gather | solution.py:171
  328.5 7.2 copy.93
  335.7 4.7 fusion
  342.7 11.7 %cholesky.273 = f32[128,128]{1,0:T(8,128)S(1)} custom-call(f32[128,128]{1,0:T(8,128)S(1)} %cholesky.705), custom_call_target="Cholesky" | custom-call | tf_op jit(solution)/shard_map/jit(cholesky)/cholesky | solution.py:172
  357.1 9.8 %custom-call.76 = f32[1,128,128]{1,2,0:T(8,128)S(1)} custom-call(f32[1,128,128]{2,1,0:T(8,128)S(1)} %get-tuple-element.210), custom_call_target="InvertDiagBlocksLowerTriangular" | custom-call | tf_op jit(solution)/shard_map/jit(cholesky)/cholesky | solution.py:172
  371.1 11.7 %cholesky.294 = f32[128,128]{1,0:T(8,128)S(1)} custom-call(f32[128,128]{1,0:T(8,128)S(1)} %cholesky.709), custom_call_target="Cholesky" | custom-call | tf_op jit(solution)/shard_map/jit(cholesky)/cholesky | solution.py:172
  383.5 10.0 %custom-call.77 = f32[1,128,128]{1,2,0:T(8,128)S(1)} custom-call(f32[1,128,128]{2,1,0:T(8,128)S(1)} %get-tuple-element.207), custom_call_target="InvertDiagBlocksLowerTriangular" | custom-call | tf_op jit(solution)/shard_map/jit(cholesky)/cholesky | solution.py:172
  397.1 11.7 %cholesky.321 = f32[128,128]{1,0:T(8,128)S(1)} custom-call(f32[128,128]{1,0:T(8,128)S(1)} %cholesky.714), custom_call_target="Cholesky" | custom-call | tf_op jit(solution)/shard_map/jit(cholesky)/cholesky | solution.py:172
  409.4 9.8 %custom-call.78 = f32[1,128,128]{1,2,0:T(8,128)S(1)} custom-call(f32[1,128,128]{2,1,0:T(8,128)S(1)} %get-tuple-element.204), custom_call_target="InvertDiagBlocksLowerTriangular" | custom-call | tf_op jit(solution)/shard_map/jit(cholesky)/cholesky | solution.py:172
  423.2 11.9 %cholesky.583 = f32[128,128]{1,0:T(8,128)S(1)} custom-call(f32[128,128]{1,0:T(8,128)S(1)} %cholesky.719), custom_call_target="Cholesky" | custom-call | tf_op jit(solution)/shard_map/jit(cholesky)/cholesky | solution.py:172
  435.7 9.8 %custom-call.79 = f32[1,128,128]{1,2,0:T(8,128)S(1)} custom-call(f32[1,128,128]{2,1,0:T(8,128)S(1)} %get-tuple-element.201), custom_call_target="InvertDiagBlocksLowerTriangular" | custom-call | tf_op jit(solution)/shard_map/jit(cholesky)/cholesky | solution.py:172
  449.3 11.7 %cholesky.602 = f32[128,128]{1,0:T(8,128)S(1)} custom-call(f32[128,128]{1,0:T(8,128)S(1)} %cholesky.724), custom_call_target="Cholesky" | custom-call | tf_op jit(solution)/shard_map/jit(cholesky)/cholesky | solution.py:172
  461.7 10.2 %custom-call.80 = f32[1,128,128]{1,2,0:T(8,128)S(1)} custom-call(f32[1,128,128]{2,1,0:T(8,128)S(1)} %get-tuple-element.198), custom_call_target="InvertDiagBlocksLowerTriangular" | custom-call | tf_op jit(solution)/shard_map/jit(cholesky)/cholesky | solution.py:172
  475.8 11.7 %cholesky.622 = f32[128,128]{1,0:T(8,128)S(1)} custom-call(f32[128,128]{1,0:T(8,128)S(1)} %cholesky.729), custom_call_target="Cholesky" | custom-call | tf_op jit(solution)/shard_map/jit(cholesky)/cholesky | solution.py:172
  488.2 9.8 %custom-call.81 = f32[1,128,128]{1,2,0:T(8,128)S(1)} custom-call(f32[1,128,128]{2,1,0:T(8,128)S(1)} %get-tuple-element.195), custom_call_target="InvertDiagBlocksLowerTriangular" | custom-call | tf_op jit(solution)/shard_map/jit(cholesky)/cholesky | solution.py:172
  501.6 11.9 %cholesky.642 = f32[128,128]{1,0:T(8,128)S(1)} custom-call(f32[128,128]{1,0:T(8,128)S(1)} %cholesky.734), custom_call_target="Cholesky" | custom-call | tf_op jit(solution)/shard_map/jit(cholesky)/cholesky | solution.py:172
  514.1 9.8 %custom-call.82 = f32[1,128,128]{1,2,0:T(8,128)S(1)} custom-call(f32[1,128,128]{2,1,0:T(8,128)S(1)} %get-tuple-element.192), custom_call_target="InvertDiagBlocksLowerTriangular" | custom-call | tf_op jit(solution)/shard_map/jit(cholesky)/cholesky | solution.py:172
  527.1 11.7 %cholesky.662 = f32[128,128]{1,0:T(8,128)S(1)} custom-call(f32[128,128]{1,0:T(8,128)S(1)} %cholesky.739), custom_call_target="Cholesky" | custom-call | tf_op jit(solution)/shard_map/jit(cholesky)/cholesky | solution.py:172
  539.5 9.8 %custom-call.83 = f32[1,128,128]{1,2,0:T(8,128)S(1)} custom-call(f32[1,128,128]{2,1,0:T(8,128)S(1)} %get-tuple-element.189), custom_call_target="InvertDiagBlocksLowerTriangular" | custom-call | tf_op jit(solution)/shard_map/jit(cholesky)/cholesky | solution.py:172
  551.9 11.9 %cholesky.680 = f32[128,128]{1,0:T(8,128)S(1)} custom-call(f32[128,128]{1,0:T(8,128)S(1)} %convolution_subtract_fusion.12), custom_call_target="Cholesky" | custom-call | tf_op jit(solution)/shard_map/jit(cholesky)/cholesky | solution.py:172
  576.1 5.2 select_select_fusion
  581.3 31.4 %while.5 = (s32[]{:T(128)}, f32[1152,1152]{1,0:T(8,128)}, s32[9,2]{0,1:T(2,128)S(1)}, f32[9,128,128]{2,1,0:T(8,128)}, s32[]{:T(128)}) while((s32[]{:T(128)}, f32[1152,1152]{1,0:T(8,128)}, s32[9,2]{0,1:T(2,128)S(1)}, f32[9,128,128]{2,1,0:T(8,128)}, s32[]{:T(128)}) %tuple.112), condition=%wide.while_cond.4, body=%wide.while_body.4.sunk | while | flops 2 | bytes 132205 | solution.py:173
  612.8 89.2 %custom-call.84 = f32[9,128,128]{1,2,0:T(8,128)S(1)} custom-call(f32[9,128,128]{2,1,0:T(8,128)} %get-tuple-element.65), custom_call_target="InvertDiagBlocksLowerTriangular" | custom-call | tf_op jit(solution)/shard_map/triangular_solve | solution.py:173
  719.5 52.8 %all-reduce.24.cloned.1.call-done = (f32[288,128]{1,0:T(8,128)}, f32[288,128]{1,0:T(8,128)}) async-done(((f32[288,128]{1,0:T(8,128)}, f32[288,128]{1,0:T(8,128)}), (f32[288,128]{1,0:T(8,128)}, f32[288,128]{1,0:T(8,128)})) %all-reduce.24.cloned.1.call-update) | async-done | bytes 294928 | tf_op jit(solution)/shard_map/psum | solution.py:180
  775.4 11.2 %all_gather.23 = f32[1152,128]{1,0:T(8,128)S(1)} all-gather(f32[288,128]{1,0:T(8,128)S(1)} %get-tuple-element.128), channel_id=1, replica_groups=mesh['group'=1,'tile'=8,'dp'=4] {'dp'}, dimensions={0}, use_global_device_ids=true | all-gather | bytes 737280 | tf_op jit(solution)/shard_map/all_gather | solution.py:195
  (213 shorter events, 135.4 us)
Async XLA Ops:
  8.0 1.0 copy-start
  8.0 27.8 %copy-start.11 = (s32[4]{0:T(128)S(1)}, s32[4]{0:T(128)}, u32[]{:S(2)}) copy-start(s32[4]{0:T(128)} %constant.530.clone) | copy-start | bytes 52
  8.0 11.1 %copy-start.5 = (bf16[1,1,24,24,128]{4,3,2,1,0:T(8,128)(2,1)S(1)}, bf16[1,1,24,24,128]{4,3,2,1,0:T(8,128)(2,1)}, u32[]{:S(2)}) copy-start(bf16[1,1,24,24,128]{4,3,2,1,0:T(8,128)(2,1)} %param.20) | copy-start | bytes 442372
  8.0 27.6 %copy-start.10 = (s32[1,4]{1,0:T(1,128)S(1)}, s32[1,4]{1,0:T(1,128)}, u32[]{:S(2)}) copy-start(s32[1,4]{1,0:T(1,128)} %param.24) | copy-start | bytes 52
  8.1 188.6 %all-reduce.18.cloned.1.call-start = ((), (), s32[]{:S(2)}) async-start(), calls=%async_computation | async-start | bytes 1179648 | tf_op jit(solution)/shard_map/psum | solution.py:138
  19.0 34.1 %copy-start.6 = (f32[144,288]{1,0:T(8,128)S(1)}, f32[144,288]{1,0:T(8,128)}, u32[]{:S(2)}) copy-start(f32[144,288]{1,0:T(8,128)} %param.26) | copy-start | bytes 497668
  53.1 146.8 %all-gather.5.cloned.1.call-start = ((), (), s32[]{:S(2)}) async-start(), calls=%async_computation.1 | async-start | bytes 2985984 | tf_op jit(solution)/shard_map/all_gather | solution.py:162
  64.6 202.1 %all-reduce.20.cloned.1.call-start = ((), (), s32[]{:S(2)}) async-start(), calls=%async_computation.2 | async-start | bytes 2654208 | tf_op jit(solution)/shard_map/psum | solution.py:168
  197.8 517.7 %copy-start.2 = (f32[1152,128]{1,0:T(8,128)}, f32[1152,128]{1,0:T(8,128)S(1)}, u32[]{:S(2)}) copy-start(f32[1152,128]{1,0:T(8,128)S(1)} %broadcast_multiply_fusion) | copy-start | bytes 1769476
  199.8 71.1 %copy-start.3 = (f32[144,1152]{1,0:T(8,128)}, f32[144,1152]{1,0:T(8,128)S(1)}, u32[]{:S(2)}) copy-start(f32[144,1152]{1,0:T(8,128)S(1)} %fusion.1) | copy-start | bytes 1990660
  203.4 72.4 %copy-start.7 = (f32[128,128]{1,0:T(8,128)S(1)}, f32[128,128]{1,0:T(8,128)}, u32[]{:S(2)}) copy-start(f32[128,128]{1,0:T(8,128)} %param.28) | copy-start | bytes 196612
  206.0 122.4 %all-gather.7.cloned.1.call-start = ((), (), s32[]{:S(2)}) async-start(), calls=%async_computation.3 | async-start | bytes 6635520 | tf_op jit(solution)/shard_map/all_gather | solution.py:171
  266.7 450.2 %all-reduce.22.cloned.1.call-start = ((), (), s32[]{:S(2)}) async-start(), calls=%async_computation.4 | async-start | bytes 147456 | tf_op jit(solution)/shard_map/psum | solution.py:178
  268.7 503.5 %all-reduce.24.cloned.1.call-start = ((), (), s32[]{:S(2)}) async-start(), calls=%async_computation.5 | async-start | bytes 589824 | tf_op jit(solution)/shard_map/psum | solution.py:180
  275.9 59.8 %copy-start.8 = (f32[128,128]{1,0:T(8,128)}, f32[128,128]{1,0:T(8,128)S(1)}, u32[]{:S(2)}) copy-start(f32[128,128]{1,0:T(8,128)S(1)} %fusion.19) | copy-start | bytes 196612
  340.4 2.3 copy-start.1
  703.6 69.9 %copy-start.9 = (f32[288,128]{1,0:T(8,128)S(1)}, f32[288,128]{1,0:T(8,128)}, u32[]{:S(2)}) copy-start(f32[288,128]{1,0:T(8,128)} %param.30) | copy-start | bytes 442372
  715.4 72.7 %copy-start.4 = (f32[1152,144]{0,1:T(8,128)}, f32[1152,144]{0,1:T(8,128)S(1)}, u32[]{:S(2)}) copy-start(f32[1152,144]{0,1:T(8,128)S(1)} %convolution_dynamic-update-slice_fusion.6) | copy-start | bytes 1990660
Sparse Core Ops, SparseCore 0:
  53.2 143.4 all-reduce.17
  266.8 61.6 all-gather.6
  331.9 40.6 all-reduce.21
Sparse Core Ops, SparseCore 1:
  64.7 35.0 all-gather.4
  206.1 60.5 all-reduce.19
  719.4 52.8 all-reduce.23
where the time goes:
time: 806 us; the launch traced here: 796 us
  other arithmetic  322 us (40%)
  waiting for transfers between devices  273 us (34%)
  matrix products  76.5 us (9%)
  blocking collectives  51.3 us (6%)
  local copies, waits for them, and re-layouts  49.5 us (6%)
  between operations  23.1 us (3%)
    another operation x35, other arithmetic, body(): lower = jnp.linalg.cholesky(gram)  196 us
    psum x1, waiting for transfers between devices, body(): summed_grad = lax.psum(partial_grad, ('tile', 'dp'))  132 us
    another operation x3, other arithmetic, body(): lax.linalg.triangular_solve(lower, power.T, left_side=True, lower=True)  94.4 us
    psum x1, waiting for transfers between devices, body(): lax.psum(lax.dot_general(power, power_cols, (((0,), (0,)), ((), ())), pre...  60.6 us
    psum x1, waiting for transfers between devices, body(): lax.psum((lax.dot_general(basis_cols, back, (((0,), (0,)), ((), ())), pre...  52.8 us
    another operation x27, local copies, waits for them, and re-layouts  31.4 us
    another operation x16, matrix products, body(): lower = jnp.linalg.cholesky(gram)  28.7 us
    all_gather x1, waiting for transfers between devices, body(): gram = lax.all_gather(gram_part, 'dp', axis=1, tiled=True)  28.1 us
  transfers between devices with their start and end apart: 6, of which 4 were waited for; matrix products, arithmetic and copies ran while one was open for 53% of the time, Pallas kernels for 0%

commit v1 on v0

--- a/solution.py
+++ b/solution.py
@@ -168,7 +168,14 @@
     gram_part = lax.psum(
         lax.dot_general(power, power_cols, (((0,), (0,)), ((), ())), precision=highest), "tile"
     )
-    gram = lax.all_gather(gram_part, "dp", axis=1, tiled=True)
+    ways, here, turn = (lax.axis_size("dp"), lax.axis_index("dp"), gram_part.shape[1])
+    line, have = (gram_part, 1)
+    while have < ways:
+        line = jnp.concatenate(
+            [line, lax.ppermute(line, "dp", [(d, (d - have) % ways) for d in range(ways)])], axis=1
+        )
+        have = 2 * have
+    gram = jnp.roll(line, here * turn, axis=1)
     lower = jnp.linalg.cholesky(gram)
     basis_new = lax.linalg.triangular_solve(lower, power.T, left_side=True, lower=True).T
     right_new = 0.95 * right_factor + 0.05 * lax.dot_general(

time: 806 us -> 856 us (1.062)
  local copies, waits for them, and re-layouts: 49.5 us -> 65.2 us
  waiting for transfers between devices: 273 us -> 287 us
  other arithmetic: 322 us -> 332 us
    ppermute x0 -> x2, waiting for transfers between devices: none -> 41.6 us  [body(): lax.ppermute(line, 'dp', [(d, (d - have) % ways) for d in range(ways)])]
    all_gather x1 -> x0, waiting for transfers between devices: 28.1 us -> none  [body(): gram = lax.all_gather(gram_part, 'dp', axis=1, tiled=True)]
    dynamic_slice x0 -> x2, local copies, waits for them, and re-layouts: none -> 9.75 us  [body(): gram = jnp.roll(line, here * turn, axis=1)]
    unnamed x38 -> x61, local copies, waits for them, and re-layouts: 5.06 us -> 14 us
  transfers between devices with their start and end apart: 6 -> 7, of which waited for: 4 -> 5; matrix products, arithmetic and copies ran while one was open for 53% -> 53% of each run, Pallas kernels for 0% -> 0%
where the time goes in v1:
time: 856 us; the launch traced here: 846 us
  other arithmetic  332 us (39%)
  waiting for transfers between devices  287 us (34%)
  matrix products  82 us (10%)
  local copies, waits for them, and re-layouts  65.2 us (8%)
  blocking collectives  51.4 us (6%)
  between operations  23.2 us (3%)
    another operation x35, other arithmetic, body(): lower = jnp.linalg.cholesky(gram)  196 us
    psum x1, waiting for transfers between devices, body(): summed_grad = lax.psum(partial_grad, ('tile', 'dp'))  132 us
    another operation x3, other arithmetic, body(): lax.linalg.triangular_solve(lower, power.T, left_side=True, lower=True)  95.3 us
    psum x1, waiting for transfers between devices, body(): lax.psum(lax.dot_general(power, power_cols, (((0,), (0,)), ((), ())), pre...  60.5 us
    psum x1, waiting for transfers between devices, body(): lax.psum((lax.dot_general(basis_cols, back, (((0,), (0,)), ((), ())), pre...  52.6 us
    ppermute x2, waiting for transfers between devices, body(): lax.ppermute(line, 'dp', [(d, (d - have) % ways) for d in range(ways)])  41.6 us
    another operation x27, local copies, waits for them, and re-layouts  31.3 us
    another operation x16, matrix products, body(): lower = jnp.linalg.cholesky(gram)  28.6 us
  transfers between devices with their start and end apart: 7, of which 5 were waited for; matrix products, arithmetic and copies ran while one was open for 53% of the time, Pallas kernels for 0%

profile of v1, /device:TPU:0, one launch (start us, length us, event | category | flops | bytes accessed | tf_op | source)
XLA Modules:
  0.0 845.7 jit_solution(15314197944084715196)
XLA Ops:
  18.5 15.9 %all_gather.16 = bf16[8,4,1,24,128]{4,3,2,1,0:T(8,128)(2,1)S(1)} all-gather(bf16[1,4,1,24,128]{4,3,2,1,0:T(8,128)(2,1)S(1)} %pad_maximum_fusion.5), channel_id=1, replica_groups=mesh['group'=1,'tile'=8,'dp'=4] {'tile'}, dimensions={0}, use_global_device_ids=true | all-gather | bytes 221184 | tf_op jit(solution)/shard_map/all_gather | solution.py:143
  35.7 14.1 %all-gather = bf16[32,1,24,128]{3,2,1,0:T(8,128)(2,1)S(1)} all-gather(bf16[4,1,24,128]{3,2,1,0:T(8,128)(2,1)S(1)} %pad_maximum_fusion.4), channel_id=2, replica_groups=mesh['group'=1,'tile'=8,'dp'=4] {'tile'}, dimensions={0}, use_global_device_ids=true | all-gather | bytes 221184 | tf_op jit(solution)/shard_map/all_gather | solution.py:130
  53.7 10.3 %all-gather.1 = bf16[4,288,144]{1,2,0:T(8,128)(2,1)S(1)} all-gather(bf16[1,288,144]{1,2,0:T(8,128)(2,1)S(1)} %bitcast_convert_fusion), channel_id=1, replica_groups=mesh['group'=1,'tile'=8,'dp'=4] {'dp'}, dimensions={0}, use_global_device_ids=true | all-gather | bytes 414720 | tf_op jit(solution)/shard_map/all_gather | solution.py:159
  65.2 132.2 %all-reduce.18.cloned.1.call-done = f32[1152,128]{1,0:T(8,128)} async-done(((f32[1152,128]{1,0:T(8,128)}), f32[1152,128]{1,0:T(8,128)}) %all-reduce.18.cloned.1.call-update) | async-done | bytes 589840 | tf_op jit(solution)/shard_map/psum | solution.py:138
  206.4 60.5 %all-reduce.20.cloned.1.call-done = f32[1152,288]{0,1:T(8,128)} async-done(((f32[1152,288]{0,1:T(8,128)}), f32[1152,288]{0,1:T(8,128)}) %all-reduce.20.cloned.1.call-update) | async-done | bytes 1327120 | tf_op jit(solution)/shard_map/psum | solution.py:168
  278.8 18.7 %collective-permute-done = f32[1152,288]{0,1:T(8,128)S(1)} collective-permute-done((f32[1152,288]{0,1:T(8,128)}, f32[1152,288]{0,1:T(8,128)S(1)}, u32[]{:S(2)}, u32[]{:S(2)}) %collective-permute-start) | collective-permute-done | bytes 1327136 | tf_op jit(solution)/shard_map/ppermute | solution.py:175
  310.0 12.5 %cholesky.693 = f32[128,128]{1,0:T(8,128)S(1)} custom-call(f32[128,128]{1,0:T(8,128)} %fusion.108), custom_call_target="Cholesky" | custom-call | tf_op jit(solution)/shard_map/jit(cholesky)/cholesky | solution.py:82
  324.6 10.6 %custom-call.85 = f32[1,128,128]{1,2,0:T(8,128)S(1)} custom-call(f32[1,128,128]{2,1,0:T(8,128)} %fusion.92), custom_call_target="InvertDiagBlocksLowerTriangular" | custom-call | tf_op jit(solution)/shard_map/triangular_solve | solution.py:83
  336.4 22.8 %collective-permute-done.1 = f32[1152,576]{0,1:T(8,128)} collective-permute-done((f32[1152,576]{0,1:T(8,128)}, f32[1152,576]{0,1:T(8,128)}, u32[]{:S(2)}, u32[]{:S(2)}) %collective-permute-start.1) | collective-permute-done | bytes 2654240 | tf_op jit(solution)/shard_map/ppermute | solution.py:175
  370.0 7.1 copy.93
  384.2 11.7 %cholesky.273 = f32[128,128]{1,0:T(8,128)S(1)} custom-call(f32[128,128]{1,0:T(8,128)S(1)} %cholesky.705), custom_call_target="Cholesky" | custom-call | tf_op jit(solution)/shard_map/jit(cholesky)/cholesky | solution.py:179
  398.6 9.8 %custom-call.76 = f32[1,128,128]{1,2,0:T(8,128)S(1)} custom-call(f32[1,128,128]{2,1,0:T(8,128)S(1)} %get-tuple-element.210), custom_call_target="InvertDiagBlocksLowerTriangular" | custom-call | tf_op jit(solution)/shard_map/jit(cholesky)/cholesky | solution.py:179
  412.6 11.7 %cholesky.294 = f32[128,128]{1,0:T(8,128)S(1)} custom-call(f32[128,128]{1,0:T(8,128)S(1)} %cholesky.709), custom_call_target="Cholesky" | custom-call | tf_op jit(solution)/shard_map/jit(cholesky)/cholesky | solution.py:179
  425.0 10.1 %custom-call.77 = f32[1,128,128]{1,2,0:T(8,128)S(1)} custom-call(f32[1,128,128]{2,1,0:T(8,128)S(1)} %get-tuple-element.207), custom_call_target="InvertDiagBlocksLowerTriangular" | custom-call | tf_op jit(solution)/shard_map/jit(cholesky)/cholesky | solution.py:179
  438.7 11.7 %cholesky.321 = f32[128,128]{1,0:T(8,128)S(1)} custom-call(f32[128,128]{1,0:T(8,128)S(1)} %cholesky.714), custom_call_target="Cholesky" | custom-call | tf_op jit(solution)/shard_map/jit(cholesky)/cholesky | solution.py:179
  451.1 9.8 %custom-call.78 = f32[1,128,128]{1,2,0:T(8,128)S(1)} custom-call(f32[1,128,128]{2,1,0:T(8,128)S(1)} %get-tuple-element.204), custom_call_target="InvertDiagBlocksLowerTriangular" | custom-call | tf_op jit(solution)/shard_map/jit(cholesky)/cholesky | solution.py:179
  464.7 11.9 %cholesky.583 = f32[128,128]{1,0:T(8,128)S(1)} custom-call(f32[128,128]{1,0:T(8,128)S(1)} %cholesky.719), custom_call_target="Cholesky" | custom-call | tf_op jit(solution)/shard_map/jit(cholesky)/cholesky | solution.py:179
  477.3 9.8 %custom-call.79 = f32[1,128,128]{1,2,0:T(8,128)S(1)} custom-call(f32[1,128,128]{2,1,0:T(8,128)S(1)} %get-tuple-element.201), custom_call_target="InvertDiagBlocksLowerTriangular" | custom-call | tf_op jit(solution)/shard_map/jit(cholesky)/cholesky | solution.py:179
  490.9 11.7 %cholesky.602 = f32[128,128]{1,0:T(8,128)S(1)} custom-call(f32[128,128]{1,0:T(8,128)S(1)} %cholesky.724), custom_call_target="Cholesky" | custom-call | tf_op jit(solution)/shard_map/jit(cholesky)/cholesky | solution.py:179
  503.3 10.0 %custom-call.80 = f32[1,128,128]{1,2,0:T(8,128)S(1)} custom-call(f32[1,128,128]{2,1,0:T(8,128)S(1)} %get-tuple-element.198), custom_call_target="InvertDiagBlocksLowerTriangular" | custom-call | tf_op jit(solution)/shard_map/jit(cholesky)/cholesky | solution.py:179
  517.1 11.7 %cholesky.622 = f32[128,128]{1,0:T(8,128)S(1)} custom-call(f32[128,128]{1,0:T(8,128)S(1)} %cholesky.729), custom_call_target="Cholesky" | custom-call | tf_op jit(solution)/shard_map/jit(cholesky)/cholesky | solution.py:179
  529.5 9.8 %custom-call.81 = f32[1,128,128]{1,2,0:T(8,128)S(1)} custom-call(f32[1,128,128]{2,1,0:T(8,128)S(1)} %get-tuple-element.195), custom_call_target="InvertDiagBlocksLowerTriangular" | custom-call | tf_op jit(solution)/shard_map/jit(cholesky)/cholesky | solution.py:179
  542.9 12.1 %cholesky.642 = f32[128,128]{1,0:T(8,128)S(1)} custom-call(f32[128,128]{1,0:T(8,128)S(1)} %cholesky.734), custom_call_target="Cholesky" | custom-call | tf_op jit(solution)/shard_map/jit(cholesky)/cholesky | solution.py:179
  555.7 9.8 %custom-call.82 = f32[1,128,128]{1,2,0:T(8,128)S(1)} custom-call(f32[1,128,128]{2,1,0:T(8,128)S(1)} %get-tuple-element.192), custom_call_target="InvertDiagBlocksLowerTriangular" | custom-call | tf_op jit(solution)/shard_map/jit(cholesky)/cholesky | solution.py:179
  568.6 11.7 %cholesky.662 = f32[128,128]{1,0:T(8,128)S(1)} custom-call(f32[128,128]{1,0:T(8,128)S(1)} %cholesky.739), custom_call_target="Cholesky" | custom-call | tf_op jit(solution)/shard_map/jit(cholesky)/cholesky | solution.py:179
  581.0 9.8 %custom-call.83 = f32[1,128,128]{1,2,0:T(8,128)S(1)} custom-call(f32[1,128,128]{2,1,0:T(8,128)S(1)} %get-tuple-element.189), custom_call_target="InvertDiagBlocksLowerTriangular" | custom-call | tf_op jit(solution)/shard_map/jit(cholesky)/cholesky | solution.py:179
  593.5 11.9 %cholesky.680 = f32[128,128]{1,0:T(8,128)S(1)} custom-call(f32[128,128]{1,0:T(8,128)S(1)} %slice_subtract_fusion.7), custom_call_target="Cholesky" | custom-call | tf_op jit(solution)/shard_map/jit(cholesky)/cholesky | solution.py:179
  617.6 5.3 select_select_fusion
  622.9 31.3 %while.5 = (s32[]{:T(128)}, f32[1152,1152]{1,0:T(8,128)}, s32[9,2]{0,1:T(2,128)S(1)}, f32[9,128,128]{2,1,0:T(8,128)}, s32[]{:T(128)}) while((s32[]{:T(128)}, f32[1152,1152]{1,0:T(8,128)}, s32[9,2]{0,1:T(2,128)S(1)}, f32[9,128,128]{2,1,0:T(8,128)}, s32[]{:T(128)}) %tuple.112), condition=%wide.while_cond.4, body=%wide.while_body.4.sunk | while | flops 2 | bytes 132205 | solution.py:180
  654.3 90.0 %custom-call.84 = f32[9,128,128]{1,2,0:T(8,128)} custom-call(f32[9,128,128]{2,1,0:T(8,128)} %get-tuple-element.65), custom_call_target="InvertDiagBlocksLowerTriangular" | custom-call | tf_op jit(solution)/shard_map/triangular_solve | solution.py:180
  769.4 52.6 %all-reduce.24.cloned.1.call-done = (f32[288,128]{1,0:T(8,128)}, f32[288,128]{1,0:T(8,128)}) async-done(((f32[288,128]{1,0:T(8,128)}, f32[288,128]{1,0:T(8,128)}), (f32[288,128]{1,0:T(8,128)}, f32[288,128]{1,0:T(8,128)})) %all-reduce.24.cloned.1.call-update) | async-done | bytes 294928 | tf_op jit(solution)/shard_map/psum | solution.py:187
  825.1 11.2 %all_gather.19 = f32[1152,128]{1,0:T(8,128)S(1)} all-gather(f32[288,128]{1,0:T(8,128)S(1)} %get-tuple-element.128), channel_id=1, replica_groups=mesh['group'=1,'tile'=8,'dp'=4] {'dp'}, dimensions={0}, use_global_device_ids=true | all-gather | bytes 737280 | tf_op jit(solution)/shard_map/all_gather | solution.py:202
  (240 shorter events, 173.6 us)
Async XLA Ops:
  8.0 1.0 copy-start
  8.0 27.2 %copy-start.20 = (s32[4]{0:T(128)S(1)}, s32[4]{0:T(128)}, u32[]{:S(2)}) copy-start(s32[4]{0:T(128)} %constant.547.clone) | copy-start | bytes 52
  8.0 10.4 %copy-start.11 = (bf16[1,1,24,24,128]{4,3,2,1,0:T(8,128)(2,1)S(1)}, bf16[1,1,24,24,128]{4,3,2,1,0:T(8,128)(2,1)}, u32[]{:S(2)}) copy-start(bf16[1,1,24,24,128]{4,3,2,1,0:T(8,128)(2,1)} %param.20) | copy-start | bytes 442372
  8.0 27.0 %copy-start.19 = (s32[1,4]{1,0:T(1,128)S(1)}, s32[1,4]{1,0:T(1,128)}, u32[]{:S(2)}) copy-start(s32[1,4]{1,0:T(1,128)} %param.24) | copy-start | bytes 52
  8.1 189.4 %all-reduce.18.cloned.1.call-start = ((), (), s32[]{:S(2)}) async-start(), calls=%async_computation | async-start | bytes 1179648 | tf_op jit(solution)/shard_map/psum | solution.py:138
  18.3 252.2 %copy-start.13 = (f32[1,26,26,128]{3,2,1,0:T(8,128)}, f32[1,26,26,128]{3,2,1,0:T(8,128)S(1)}, u32[]{:S(2)}) copy-start(f32[1,26,26,128]{3,2,1,0:T(8,128)S(1)} %get-tuple-element.131) | copy-start | bytes 1038340
  18.3 35.3 %copy-start.14 = (f32[144,288]{1,0:T(8,128)S(1)}, f32[144,288]{1,0:T(8,128)}, u32[]{:S(2)}) copy-start(f32[144,288]{1,0:T(8,128)} %param.26) | copy-start | bytes 497668
  50.5 148.0 %copy-start.15 = (f32[144,1152]{1,0:T(8,128)S(1)}, f32[144,1152]{1,0:T(8,128)}, u32[]{:S(2)}) copy-start(f32[144,1152]{1,0:T(8,128)} %param.25) | copy-start | bytes 1990660
  51.0 1.1 copy-start.8
  53.6 145.8 %all-gather.4.cloned.1.call-start = ((), (), s32[]{:S(2)}) async-start(), calls=%async_computation.1 | async-start | bytes 2985984 | tf_op jit(solution)/shard_map/all_gather | solution.py:162
  65.2 204.1 %copy-start.18 = (f32[288,128]{1,0:T(8,128)S(1)}, f32[288,128]{1,0:T(8,128)}, u32[]{:S(2)}) copy-start(f32[288,128]{1,0:T(8,128)} %param.29) | copy-start | bytes 442372
  65.2 201.7 %all-reduce.20.cloned.1.call-start = ((), (), s32[]{:S(2)}) async-start(), calls=%async_computation.2 | async-start | bytes 2654208 | tf_op jit(solution)/shard_map/psum | solution.py:168
  198.6 566.7 %copy-start.5 = (f32[1152,128]{1,0:T(8,128)}, f32[1152,128]{1,0:T(8,128)S(1)}, u32[]{:S(2)}) copy-start(f32[1152,128]{1,0:T(8,128)S(1)} %broadcast_multiply_fusion) | copy-start | bytes 1769476
  199.3 72.0 %copy-start.9 = (f32[144,1152]{1,0:T(8,128)}, f32[144,1152]{1,0:T(8,128)S(1)}, u32[]{:S(2)}) copy-start(f32[144,1152]{1,0:T(8,128)S(1)} %fusion.1) | copy-start | bytes 1990660
  202.9 0.8 copy-start.6
  206.4 560.4 %all-reduce.22.cloned.1.call-start = ((), (), s32[]{:S(2)}) async-start(), calls=%async_computation.3 | async-start | bytes 147456 | tf_op jit(solution)/shard_map/psum | solution.py:185
  266.9 30.7 %collective-permute-start = (f32[1152,288]{0,1:T(8,128)}, f32[1152,288]{0,1:T(8,128)S(1)}, u32[]{:S(2)}, u32[]{:S(2)}) collective-permute-start(f32[1152,288]{0,1:T(8,128)} %all-reduce.20.cloned.1.call-done), channel_id=1, source_target_pairs={{0,3},{1,0},{2,1},{3,2},{4,7},{5,4},{6,5},{7,6},{8,11},{9,8},{10,9... | collective-permute-start | bytes 3981320 | tf_op jit(solution)/shard_map/ppermute | solution.py:175
  270.3 37.0 %copy-start.16 = (f32[128,128]{1,0:T(8,128)S(1)}, f32[128,128]{1,0:T(8,128)}, u32[]{:S(2)}) copy-start(f32[128,128]{1,0:T(8,128)} %param.28) | copy-start | bytes 196612
  270.3 551.7 %all-reduce.24.cloned.1.call-start = ((), (), s32[]{:S(2)}) async-start(), calls=%async_computation.4 | async-start | bytes 589824 | tf_op jit(solution)/shard_map/psum | solution.py:187
  271.3 64.9 %copy-start.4 = (f32[1152,288]{0,1:T(8,128)S(1)}, f32[1152,288]{0,1:T(8,128)}, u32[]{:S(2)}) copy-start(f32[1152,288]{0,1:T(8,128)} %all-reduce.20.cloned.1.call-done) | copy-start | bytes 3981316
  278.8 23.2 %copy-start.12 = (f32[1,24,24,128]{3,1,2,0:T(8,128)S(1)}, f32[1,24,24,128]{3,1,2,0:T(8,128)}, u32[]{:S(2)}) copy-start(f32[1,24,24,128]{3,1,2,0:T(8,128)} %fusion.136) | copy-start | bytes 884740
  300.6 58.7 %collective-permute-start.1 = (f32[1152,576]{0,1:T(8,128)}, f32[1152,576]{0,1:T(8,128)}, u32[]{:S(2)}, u32[]{:S(2)}) collective-permute-start(f32[1152,576]{0,1:T(8,128)} %pad_maximum_fusion), channel_id=1, source_target_pairs={{0,2},{1,3},{2,0},{3,1},{4,6},{5,7},{6,4},{7,5},{8,10},{9,11},{10,... | collective-permute-start | bytes 7962632 | tf_op jit(solution)/shard_map/ppermute | solution.py:175
  307.3 17.2 %copy-start.17 = (f32[128,128]{1,0:T(8,128)}, f32[128,128]{1,0:T(8,128)S(1)}, u32[]{:S(2)}) copy-start(f32[128,128]{1,0:T(8,128)S(1)} %fusion.11) | copy-start | bytes 196612
  363.3 4.0 copy-start.2
  381.9 2.3 copy-start.3
  617.6 126.7 %copy-start.7 = (f32[144,1152]{1,0:T(8,128)S(1)}, f32[144,1152]{1,0:T(8,128)}, u32[]{:S(2)}) copy-start(f32[144,1152]{1,0:T(8,128)} %copy-done.6) | copy-start | bytes 1990660
  753.6 84.3 %copy-start.1 = (bf16[1,1,24,24,128]{4,3,2,1,0:T(8,128)(2,1)S(1)}, bf16[1,1,24,24,128]{4,3,2,1,0:T(8,128)(2,1)}, u32[]{:S(2)}) copy-start(bf16[1,1,24,24,128]{4,3,2,1,0:T(8,128)(2,1)} %param.21) | copy-start | bytes 442372
  765.3 72.6 %copy-start.10 = (f32[1152,144]{0,1:T(8,128)}, f32[1152,144]{0,1:T(8,128)S(1)}, u32[]{:S(2)}) copy-start(f32[1152,144]{0,1:T(8,128)S(1)} %convolution_dynamic-update-slice_fusion.6) | copy-start | bytes 1990660
Sparse Core Ops, SparseCore 0:
  53.7 143.7 all-reduce.17
  270.4 58.9 all-reduce.21
Sparse Core Ops, SparseCore 1:
  65.3 35.0 all-gather.3
  206.4 60.4 all-reduce.19
  769.2 52.7 all-reduce.23
